TPU v7x, 32 devices: a whole 2x2x4 slice. The times are simulated.
32 devices in a mesh: fsdp: 4 (over y, x), ctx: 4 (over z), tp: 2 (over core).
Axes of the slice: x: 2, y: 2, z: 4, core: 2. Of those that a mesh axis runs over, the one named last changes fastest.
Arguments:
- tokens: bfloat16 [4, 2048, 1024], P('fsdp', 'ctx'), may hold values from -6 to 6
- segment_ids: int32 [4, 2048], P('fsdp', 'ctx'), may hold values from 0 to 10, as said below
- positions: int32 [4, 2048], P('fsdp', 'ctx'), may hold values from 0 to 2047, as said below
- attention_gain: bfloat16 [1024], P('fsdp'), may hold values from 0.099609375 to 1.8984375
- attention_shift: bfloat16 [1024], P('fsdp'), may hold values from -1.75 to 1.75
- feedforward_gain: bfloat16 [1024], P('fsdp'), may hold values from 0.099609375 to 1.8984375
- feedforward_shift: bfloat16 [1024], P('fsdp'), may hold values from -1.75 to 1.75
- joint_weight: bfloat16 [1024, 3, 1024], P('fsdp', None, 'tp'), may hold values from -8 to 8
- joint_bias: bfloat16 [3, 1024], P(None, ('tp', 'fsdp')), may hold values from -3 to 3
- output_weight: bfloat16 [1024, 1024], P('tp', 'fsdp'), may hold values from -1.5 to 1.5
- output_bias: bfloat16 [1024], P('fsdp'), may hold values from -1.75 to 1.75
- up_weight: bfloat16 [1024, 4096], P('fsdp', 'tp'), may hold values from -0.1875 to 0.1875
- up_bias: bfloat16 [4096], P(('tp', 'fsdp')), may hold values from -3 to 3
- down_weight: bfloat16 [4096, 1024], P('tp', 'fsdp'), may hold values from -0.09375 to 0.09375
- down_bias: bfloat16 [1024], P('fsdp'), may hold values from -1.75 to 1.75
- cotangent: float32 [4, 2048, 1024], P('fsdp', 'ctx'), may hold values from -6 to 6
Outputs:
- result: float32 [4, 2048, 1024], P('fsdp', 'ctx')
- tokens_grad: float32 [4, 2048, 1024], P('fsdp', 'ctx')
- attention_gain_grad: float32 [1024], P('fsdp')
- attention_shift_grad: float32 [1024], P('fsdp')
- feedforward_gain_grad: float32 [1024], P('fsdp')
- feedforward_shift_grad: float32 [1024], P('fsdp')
- joint_weight_grad: float32 [1024, 3, 1024], P('fsdp', None, 'tp')
- joint_bias_grad: float32 [3, 1024], P(None, ('tp', 'fsdp'))
- output_weight_grad: float32 [1024, 1024], P('tp', 'fsdp')
- output_bias_grad: float32 [1024], P('fsdp')
- up_weight_grad: float32 [1024, 4096], P('fsdp', 'tp')
- up_bias_grad: float32 [4096], P(('tp', 'fsdp'))
- down_weight_grad: float32 [4096, 1024], P('tp', 'fsdp')
- down_bias_grad: float32 [1024], P('fsdp')
Inputs may be any that keep to these rules, and one draw needn't show every extreme that they name: `segment_ids`: along each sequence the ids start at 0 and rise by one at each document's first token; a document holds 204 to 2048 tokens, the last one cut at the sequence's end. The first sequence is one document; the last sequence is documents of 204 tokens. `positions`: each token's offset from the first token of its document; the first sequence is one document.
All inputs are finite; a program needn't handle non-finite values.
Results may differ from a plain program's by a relative error of at most 0.011.
Values may be sent and summed in bfloat16 or wider, within the bound.
No kernel may reach another device: no remote copies, remote signals or barrier semaphores. Data moves between devices by JAX's collectives and lax.ppermute only.
A program may use at most 192 MiB of HBM per device.

v0:
```python
import jax
import jax.numpy as jnp
from jax import lax
from jax.sharding import PartitionSpec as P

HD = 64
ROT = 16
EPS = 1e-05
ROPE_BASE = 10000.0


def rope_tables(offsets):
    half_dim = ROT // 2
    freq = ROPE_BASE ** (-(jnp.arange(half_dim, dtype=jnp.float32) * 2.0 / ROT))
    angle = offsets.astype(jnp.float32)[:, None] * freq[None, :]
    return (jnp.cos(angle)[:, None, :], jnp.sin(angle)[:, None, :])


def rotate(tensor, cosine, sine):
    half_dim = ROT // 2
    front = tensor[..., :half_dim]
    middle = tensor[..., half_dim:ROT]
    return jnp.concatenate(
        [front * cosine - middle * sine, middle * cosine + front * sine, tensor[..., ROT:]], axis=-1
    )


def unrotate(grads, cosine, sine):
    half_dim = ROT // 2
    front = grads[..., :half_dim]
    middle = grads[..., half_dim:ROT]
    return jnp.concatenate(
        [front * cosine + middle * sine, middle * cosine - front * sine, grads[..., ROT:]], axis=-1
    )


def normalize(rows):
    center = jnp.mean(rows, -1, keepdims=True)
    centred = rows - center
    spread = jnp.mean(centred * centred, -1, keepdims=True)
    rstd = lax.rsqrt(spread + EPS)
    return (centred * rstd, rstd)


def norm_back(upstream, normed, rstd, gain):
    scaled = upstream * gain
    return rstd * (
        scaled
        - jnp.mean(scaled, -1, keepdims=True)
        - normed * jnp.mean(scaled * normed, -1, keepdims=True)
    )


def masked_scores(query_blk, query_index, query_seg, keys, key_seg):
    scores = jnp.einsum(
        "qhe,khe->hqk", query_blk, keys, preferred_element_type=jnp.float32
    ) * HD ** (-0.5)
    key_index = jnp.arange(keys.shape[0], dtype=jnp.int32)
    allowed = (key_seg[None, :] == query_seg[:, None]) & (
        key_index[None, :] <= query_index[:, None]
    )
    return jnp.where(allowed[None], scores, -jnp.inf)


def local(
    tokens,
    segment_ids,
    positions,
    attention_gain,
    attention_shift,
    feedforward_gain,
    feedforward_shift,
    joint_weight,
    joint_bias,
    output_weight,
    output_bias,
    up_weight,
    up_bias,
    down_weight,
    down_bias,
    cotangent,
):
    f32 = jnp.float32
    bf16 = jnp.bfloat16
    scale = HD ** (-0.5)
    small = jnp.stack(
        [
            attention_gain,
            attention_shift,
            feedforward_gain,
            feedforward_shift,
            output_bias,
            down_bias,
        ]
    )
    full_joint, full_output, full_up, full_down, full_small, full_jbias, full_upbias = (
        lax.all_gather(joint_weight, "fsdp", axis=0, tiled=True),
        lax.all_gather(output_weight, "fsdp", axis=1, tiled=True),
        lax.all_gather(up_weight, "fsdp", axis=0, tiled=True),
        lax.all_gather(down_weight, "fsdp", axis=1, tiled=True),
        lax.all_gather(small, "fsdp", axis=1, tiled=True),
        lax.all_gather(joint_bias, "fsdp", axis=1, tiled=True),
        lax.all_gather(up_bias, "fsdp", axis=0, tiled=True),
    )
    params = full_small.astype(f32)
    gain_one = params[0]
    shift_one = params[1]
    gain_two = params[2]
    shift_two = params[3]
    rows = tokens[0].astype(f32)
    count_rows = rows.shape[0]
    local_width = joint_weight.shape[2]
    heads_here = local_width // HD
    normed, rstd = normalize(rows)
    first = (normed * gain_one + shift_one).astype(bf16)
    second = (normed * gain_two + shift_two).astype(bf16)
    joint = (
        jnp.einsum("nd,dpe->npe", first, full_joint, preferred_element_type=f32)
        + full_jbias.astype(f32)[None]
    )
    cosine, sine = rope_tables(positions[0])
    queries = rotate(joint[:, 0].reshape(count_rows, heads_here, HD), cosine, sine).astype(bf16)
    keys_here = rotate(joint[:, 1].reshape(count_rows, heads_here, HD), cosine, sine).astype(bf16)
    values_here = joint[:, 2].reshape(count_rows, heads_here, HD).astype(bf16)
    seg_here = segment_ids[0]
    all_keys, all_values, all_segs = (
        lax.all_gather(keys_here, "ctx", axis=0, tiled=True),
        lax.all_gather(values_here, "ctx", axis=0, tiled=True),
        lax.all_gather(seg_here.astype(bf16), "ctx", axis=0, tiled=True),
    )
    key_seg = all_segs.astype(f32)
    query_seg = seg_here.astype(f32)
    query_index = lax.axis_index("ctx") * count_rows + jnp.arange(count_rows, dtype=jnp.int32)
    block = min(512, count_rows)
    count_blocks = count_rows // block
    query_blocks = queries.reshape(count_blocks, block, heads_here, HD)
    index_blocks = query_index.reshape(count_blocks, block)
    seg_blocks = query_seg.reshape(count_blocks, block)

    def forward_block(args):
        query_blk, block_index, block_seg = args
        scores = masked_scores(query_blk, block_index, block_seg, all_keys, key_seg)
        top = jnp.max(scores, -1, keepdims=True)
        lse = top + jnp.log(jnp.sum(jnp.exp(scores - top), -1, keepdims=True))
        probs = jnp.exp(scores - lse).astype(bf16)
        mixed = jnp.einsum("hqk,khe->qhe", probs, all_values, preferred_element_type=f32)
        return (mixed, lse[..., 0])

    context32, lse_all = lax.map(forward_block, (query_blocks, index_blocks, seg_blocks))
    context32 = context32.reshape(count_rows, local_width)
    context = context32.astype(bf16)
    upper = jnp.dot(second, full_up, preferred_element_type=f32) + full_upbias.astype(f32)
    activated = jax.nn.gelu(upper, approximate=False).astype(bf16)
    partial_value = jnp.dot(context, full_output, preferred_element_type=f32) + jnp.dot(
        activated, full_down, preferred_element_type=f32
    )
    mixed_all = lax.psum(partial_value, "tp")
    result = rows + mixed_all + params[4] + params[5]
    back_joint, back_output, back_up, back_down = (
        lax.all_gather(joint_weight, "fsdp", axis=0, tiled=True),
        lax.all_gather(output_weight, "fsdp", axis=1, tiled=True),
        lax.all_gather(up_weight, "fsdp", axis=0, tiled=True),
        lax.all_gather(down_weight, "fsdp", axis=1, tiled=True),
    )
    cot = cotangent[0]
    cot_b = cot.astype(bf16)
    grad_output_w = jnp.dot(context.T, cot_b, preferred_element_type=f32)
    bias_sum = jnp.sum(cot, 0)
    grad_down_w = jnp.dot(activated.T, cot_b, preferred_element_type=f32)
    d_act = jnp.einsum("nd,fd->nf", cot_b, back_down, preferred_element_type=f32)
    unused, gelu_back = jax.vjp(lambda value: jax.nn.gelu(value, approximate=False), upper)
    d_upper = gelu_back(d_act)[0]
    d_upper_b = d_upper.astype(bf16)
    grad_up_w = jnp.dot(second.T, d_upper_b, preferred_element_type=f32)
    grad_up_b = jnp.sum(d_upper, 0)
    d_second_part = jnp.einsum("nf,df->nd", d_upper_b, back_up, preferred_element_type=f32)
    d_context = (
        jnp.einsum("nd,wd->nw", cot_b, back_output, preferred_element_type=f32)
        .astype(bf16)
        .reshape(count_rows, heads_here, HD)
    )
    delta = jnp.sum(d_context.astype(f32) * context32.reshape(count_rows, heads_here, HD), -1)
    dctx_blocks = d_context.reshape(count_blocks, block, heads_here, HD)

    def backward_block(args):
        query_blk, block_index, block_seg, dctx_blk, delta_blk, lse_blk = args
        scores = masked_scores(query_blk, block_index, block_seg, all_keys, key_seg)
        probs = jnp.exp(scores - lse_blk[..., None]).astype(bf16)
        d_probs = jnp.einsum("qhe,khe->hqk", dctx_blk, all_values, preferred_element_type=f32)
        d_scores = (probs.astype(f32) * (d_probs - jnp.transpose(delta_blk)[..., None])).astype(
            bf16
        )
        d_query_blk = (
            jnp.einsum("hqk,khe->qhe", d_scores, all_keys, preferred_element_type=f32) * scale
        )
        return (probs, d_scores, d_query_blk)

    probs_all, dscores_all, d_queries = lax.map(
        backward_block,
        (
            query_blocks,
            index_blocks,
            seg_blocks,
            dctx_blocks,
            delta.reshape(count_blocks, block, heads_here),
            lse_all,
        ),
    )
    d_queries = d_queries.reshape(count_rows, heads_here, HD)
    key_part = (
        jnp.einsum("bhqk,bqhe->khe", dscores_all, query_blocks, preferred_element_type=f32) * scale
    )
    value_part = jnp.einsum("bhqk,bqhe->khe", probs_all, dctx_blocks, preferred_element_type=f32)
    key_value = lax.psum_scatter(
        jnp.concatenate(
            [
                key_part.reshape(count_rows * lax.axis_size("ctx"), local_width),
                value_part.reshape(count_rows * lax.axis_size("ctx"), local_width),
            ],
            axis=1,
        ),
        "ctx",
        scatter_dimension=0,
        tiled=True,
    )
    d_keys = key_value[:, :local_width].reshape(count_rows, heads_here, HD)
    d_values = key_value[:, local_width:]
    d_joint = jnp.stack(
        [
            unrotate(d_queries, cosine, sine).reshape(count_rows, local_width),
            unrotate(d_keys, cosine, sine).reshape(count_rows, local_width),
            d_values,
        ],
        axis=1,
    )
    d_joint_b = d_joint.astype(bf16)
    grad_joint_w = jnp.einsum("nd,npe->dpe", first, d_joint_b, preferred_element_type=f32)
    grad_joint_b = jnp.sum(d_joint, 0)
    d_first_part = jnp.einsum("npe,dpe->nd", d_joint_b, back_joint, preferred_element_type=f32)
    d_first, d_second = lax.psum((d_first_part, d_second_part), "tp")
    norm_stats = jnp.stack(
        [
            jnp.sum(d_first * normed, 0),
            jnp.sum(d_first, 0),
            jnp.sum(d_second * normed, 0),
            jnp.sum(d_second, 0),
        ]
    )
    tokens_grad = (
        cot
        + norm_back(d_first, normed, rstd, gain_one)
        + norm_back(d_second, normed, rstd, gain_two)
    )
    grad_small = jnp.concatenate([norm_stats, bias_sum[None], bias_sum[None]], axis=0)
    share_joint, share_output, share_up, share_down, share_small, share_jbias, share_upbias = (
        lax.psum_scatter(grad_joint_w, ("fsdp", "ctx"), scatter_dimension=0, tiled=True),
        lax.psum_scatter(grad_output_w, ("fsdp", "ctx"), scatter_dimension=1, tiled=True),
        lax.psum_scatter(grad_up_w, ("fsdp", "ctx"), scatter_dimension=0, tiled=True),
        lax.psum_scatter(grad_down_w, ("fsdp", "ctx"), scatter_dimension=1, tiled=True),
        lax.psum_scatter(grad_small, ("fsdp", "ctx"), scatter_dimension=1, tiled=True),
        lax.psum_scatter(grad_joint_b, ("fsdp", "ctx"), scatter_dimension=1, tiled=True),
        lax.psum_scatter(grad_up_b, ("fsdp", "ctx"), scatter_dimension=0, tiled=True),
    )
    owned = (
        lax.all_gather(share_joint, "ctx", axis=0, tiled=True),
        lax.all_gather(share_output, "ctx", axis=1, tiled=True),
        lax.all_gather(share_up, "ctx", axis=0, tiled=True),
        lax.all_gather(share_down, "ctx", axis=1, tiled=True),
        lax.all_gather(share_small, "ctx", axis=1, tiled=True),
        lax.all_gather(share_jbias, "ctx", axis=1, tiled=True),
        lax.all_gather(share_upbias, "ctx", axis=0, tiled=True),
    )
    owned_joint, owned_output, owned_up, owned_down, owned_small, owned_jbias, owned_upbias = owned
    return (
        result[None],
        tokens_grad[None],
        owned_small[0],
        owned_small[1],
        owned_small[2],
        owned_small[3],
        owned_joint,
        owned_jbias,
        owned_output,
        owned_small[4],
        owned_up,
        owned_upbias,
        owned_down,
        owned_small[5],
    )


def solution(mesh):
    placed = (
        P("fsdp", "ctx", None),
        P("fsdp", "ctx"),
        P("fsdp", "ctx"),
        P("fsdp"),
        P("fsdp"),
        P("fsdp"),
        P("fsdp"),
        P("fsdp", None, "tp"),
        P(None, ("tp", "fsdp")),
        P("tp", "fsdp"),
        P("fsdp"),
        P("fsdp", "tp"),
        P(("tp", "fsdp")),
        P("tp", "fsdp"),
        P("fsdp"),
        P("fsdp", "ctx", None),
    )
    return jax.shard_map(
        local,
        mesh=mesh,
        in_specs=placed,
        out_specs=(
            P("fsdp", "ctx", None),
            P("fsdp", "ctx", None),
            P("fsdp"),
            P("fsdp"),
            P("fsdp"),
            P("fsdp"),
            P("fsdp", None, "tp"),
            P(None, ("tp", "fsdp")),
            P("tp", "fsdp"),
            P("fsdp"),
            P("fsdp", "tp"),
            P(("tp", "fsdp")),
            P("tp", "fsdp"),
            P("fsdp"),
        ),
        check_vma=False,
    )
```

profile of v0, /device:TPU:0, one launch (start us, length us, event | category | flops | bytes accessed | tf_op | source)
XLA Modules:
  0.0 1352.6 jit_solution(17469226401049093940)
XLA Ops:
  7.3 2.4 copy.51
  10.5 1.4 convert_reduce_fusion
  12.7 9.5 all_gather.57
  22.3 8.3 all_gather.55
  31.2 26.0 %all-gather.15.cloned.1.call-done = bf16[1024,3,512]{0,2,1:T(8,128)(2,1)} async-done(((bf16[256,3,512]{0,2,1:T(8,128)(2,1)}), bf16[1024,3,512]{0,2,1:T(8,128)(2,1)}) %all-gather.15.cloned.1.call-update) | async-done | bytes 3145744 | tf_op jit(solution)/shard_map/all_gather | solution.py:97
  57.2 3.9 convolution_add_fusion
  64.1 2.1 slice.168
  67.5 11.9 all-gather
  80.6 4.9 all-gather.21.cloned.1.call-done
  85.5 2.8 fusion.75
  89.5 44.2 %all-gather.19.cloned.1.call-done = bf16[2048,8,64]{0,2,1:T(8,128)(2,1)} async-done(((bf16[512,8,64]{0,2,1:T(8,128)(2,1)}), bf16[2048,8,64]{0,2,1:T(8,128)(2,1)}) %all-gather.19.cloned.1.call-update) | async-done | bytes 2097168 | tf_op jit(solution)/shard_map/all_gather | solution.py:127
  133.6 16.0 %fusion = (f32[8,512]{1,0:T(8,128)S(1)}, f32[8,512,2048]{2,1,0:T(8,128)}) fusion(pred[512,2048]{1,0:T(8,128)(4,1)S(1)} %fusion.7, bf16[2048,8,64]{0,2,1:T(8,128)(2,1)} %all-gather.19.cloned.1.call-done, bf16[512,8,48]{0,2,1:T(8,128)(2,1)S(1)} %slice.170, bf16[512,8,8]{0,2,1:T(8,128)(2,1)} %get-tuple-element.148, bf16[512,8,8]{0,2,1:T(8,128)(2,1)} %get-tuple-element.147), kind=kOutput, calls=%fused_computation.4 | convolution fusion | flops 1100476416 | bytes 37240832 | tf_op jit(solution)/shard_map/while/body/eval_jaxpr/qhe,khe->hqk/dot_general | solution.py:55
  149.6 15.9 %exponential_reduce_fusion = f32[8,512]{1,0:T(8,128)S(1)} fusion(f32[8,512,2048]{2,1,0:T(8,128)} %get-tuple-element.176, f32[8,512]{1,0:T(8,128)S(1)} %get-tuple-element.175, pred[512,2048]{1,0:T(8,128)(4,1)S(1)} %fusion.7), kind=kLoop, calls=%fused_computation.2 | loop fusion | flops 33550336 | bytes 34635776 | tf_op jit(solution)/shard_map/while/body/eval_jaxpr/reduce_sum | solution.py:144
  165.5 4.6 copy-done
  170.1 9.4 exponential_convert_fusion
  180.3 12.4 multiply_reduce_fusion.2
  192.7 25.3 %multiply_convert_fusion = bf16[8,512,2048]{2,1,0:T(8,128)(2,1)} fusion(bf16[8,512,2048]{2,1,0:T(8,128)(2,1)} %exponential_convert_fusion, bf16[512,8,64]{0,2,1:T(8,128)(2,1)S(1)} %bitcast.212, bf16[2048,8,64]{0,2,1:T(8,128)(2,1)} %all-gather.17.cloned.1.call-done, f32[8,512]{1,0:T(8,128)S(1)} %bitcast.227), kind=kOutput, calls=%fused_computation | convolution fusion | flops 1107296256 | bytes 36192256 | tf_op jit(solution)/shard_map/while/body/eval_jaxpr/qhe,khe->hqk/dot_general | solution.py:189
  218.1 10.9 convolution_multiply_fusion
  228.9 5.4 copy.52
  234.3 10.9 fusion.82
  245.2 5.4 copy.53
  250.6 8.2 pad_maximum_fusion
  259.4 8.0 all-gather.1
  267.5 15.1 %multiply_convert_fusion.1 = (bf16[512,2048]{1,0:T(8,128)(2,1)}, f32[512,2048]{1,0:T(8,128)}, f32[512,2048]{1,0:T(8,128)}) fusion(f32[2048]{0:T(1024)S(1)} %bitcast.253, bf16[1024,2048]{1,0:T(8,128)(2,1)} %all-gather.23.cloned.1.call-done, bf16[1,512,1024]{2,1,0:T(8,128)(2,1)S(1)} %copy-done.3, f32[1024]{0:T(1024)S(1)} %bitcast.257, f32[1024]{0:T(1024)S(1)} %bitcast.234, ...), kind=kOutput, calls=%fused_computation.9 | convolution fusion | flops 2219835392 | bytes 15749120 | tf_op jit(solution)/shard_map/dot_general | solution.py:152
  282.6 5.2 all-gather.25.cloned.1.call-done
  287.8 7.4 fusion.72
  295.2 1.3 copy-done.32
  296.6 5.8 fusion.46
  302.5 7.2 fusion.73
  310.2 6.7 fusion.81
  316.9 3.7 fusion.48
  320.6 12.7 fusion.41
  333.2 2.1 slice.136
  335.3 4.2 convolution_add_fusion.1
  339.6 95.1 %reduce-scatter.12.cloned.1.call-done = f32[512,1024]{1,0:T(8,128)} async-done(((f32[2048,1024]{1,0:T(8,128)}), f32[512,1024]{1,0:T(8,128)}) %reduce-scatter.12.cloned.1.call-update) | async-done | bytes 2097168 | tf_op jit(solution)/shard_map/reduce_scatter | solution.py:214
  434.6 3.0 fusion.68
  437.7 2.5 copy.54
  442.6 2.8 pad_maximum_fusion.2
  445.4 2.6 copy.55
  448.0 2.5 copy.56
  450.5 6.0 convolution_bitcast_fusion
  457.2 6.6 fusion.55
  463.9 3.1 fusion.43
  467.1 2.1 fusion.20
  470.1 149.9 %reduce-scatter.18.cloned.1.call-done = f32[64,2048]{1,0:T(8,128)} async-done(((f32[1024,2048]{1,0:T(8,128)}), f32[64,2048]{1,0:T(8,128)}) %reduce-scatter.18.cloned.1.call-update) | async-done | bytes 524304 | tf_op jit(solution)/shard_map/reduce_scatter | solution.py:258
  620.1 182.1 %reduce-scatter.20.cloned.1.call-done = f32[2048,64]{0,1:T(8,128)} async-done(((f32[2048,1024]{0,1:T(8,128)}), f32[2048,64]{0,1:T(8,128)}) %reduce-scatter.20.cloned.1.call-update) | async-done | bytes 524304 | tf_op jit(solution)/shard_map/reduce_scatter | solution.py:259
  802.4 33.3 %all-reduce.4.cloned.1.call-done = (f32[512,1024]{1,0:T(8,128)}, f32[512,1024]{1,0:T(8,128)}, f32[512,1024]{1,0:T(8,128)}) async-done(((f32[512,1024]{1,0:T(8,128)}, f32[512,1024]{1,0:T(8,128)}, f32[512,1024]{1,0:T(8,128)}), (f32[512,1024]{1,0:T(8,128)}, f32[512,1024]{1,0:T(8,128)}, f32[512,1024]{1,0:T(8,128)})) %all-reduce.4.cloned.1.call-update) | async-done | bytes 6291472 | tf_op jit(solution)/shard_map/psum | solution.py:157
  835.7 3.4 fusion.35
  840.2 137.3 %reduce-scatter.14.cloned.1.call-done = f32[64,3,512]{2,0,1:T(8,128)} async-done(((f32[1024,3,512]{2,0,1:T(8,128)}), f32[64,3,512]{2,0,1:T(8,128)}) %reduce-scatter.14.cloned.1.call-update) | async-done | bytes 393232 | tf_op jit(solution)/shard_map/reduce_scatter | solution.py:256
  978.8 39.4 %all-reduce = f32[2048]{0:T(1024)S(1)} all-reduce(f32[2048]{0:T(1024)S(1)} %get-tuple-element.179), channel_id=9, replica_groups=mesh['fsdp'=4,'ctx'=4,'tp'=2] {'fsdp','ctx'}, use_global_device_ids=true, to_apply=%region_25.26.clone | all-reduce | flops 2048 | bytes 16384
  1018.3 7.8 all-gather.4
  1026.1 36.4 %reduce-scatter.16.cloned.1.call-done = f32[512,64]{0,1:T(8,128)} async-done(((f32[512,1024]{0,1:T(8,128)}), f32[512,64]{0,1:T(8,128)}) %reduce-scatter.16.cloned.1.call-update) | async-done | bytes 131088 | tf_op jit(solution)/shard_map/reduce_scatter | solution.py:257
  1062.5 15.7 %all_gather.68 = f32[512,256]{0,1:T(8,128)} all-gather(f32[512,64]{0,1:T(8,128)} %reduce-scatter.16.cloned.1.call-done), channel_id=1, replica_groups=mesh['fsdp'=4,'ctx'=4,'tp'=2] {'ctx'}, dimensions={1}, use_global_device_ids=true | all-gather | bytes 655360 | tf_op jit(solution)/shard_map/all_gather | solution.py:266
  1078.2 2.0 copy.61
  1080.2 57.7 %reduce-scatter.24.cloned.1.call-done = f32[32,3]{1,0:T(8,128)} async-done(((f32[512,3]{1,0:T(8,128)}), f32[32,3]{1,0:T(8,128)}) %reduce-scatter.24.cloned.1.call-update) | async-done | bytes 400
  1138.7 12.2 all-gather.3
  1151.6 30.2 %all-gather.29.cloned.1.call-done = f32[256,2048]{1,0:T(8,128)} async-done(((f32[64,2048]{1,0:T(8,128)}), f32[256,2048]{1,0:T(8,128)}) %all-gather.29.cloned.1.call-update) | async-done | bytes 2097168 | tf_op jit(solution)/shard_map/all_gather | solution.py:267
  1181.7 46.1 %all-gather.31.cloned.1.call-done = f32[2048,256]{0,1:T(8,128)} async-done(((f32[2048,64]{0,1:T(8,128)}), f32[2048,256]{0,1:T(8,128)}) %all-gather.31.cloned.1.call-update) | async-done | bytes 2097168 | tf_op jit(solution)/shard_map/all_gather | solution.py:268
  1227.8 2.9 copy.62
  1230.7 4.9 fusion.31
  1235.6 70.6 %reduce-scatter.22.cloned.1.call-done = f32[64,6]{1,0:T(8,128)} async-done(((f32[1024,6]{1,0:T(8,128)}), f32[64,6]{1,0:T(8,128)}) %reduce-scatter.22.cloned.1.call-update) | async-done | bytes 1552
  1307.1 13.4 all-gather.2
  1321.1 20.2 %all-gather.27.cloned.1.call-done = f32[256,3,512]{2,0,1:T(8,128)} async-done(((f32[64,3,512]{2,0,1:T(8,128)}), f32[256,3,512]{2,0,1:T(8,128)}) %all-gather.27.cloned.1.call-update) | async-done | bytes 1572880 | tf_op jit(solution)/shard_map/all_gather | solution.py:265
  1341.3 2.7 copy.76
  (150 shorter events, 21.8 us)
Async XLA Ops:
  7.2 4.8 copy-start.2
  7.2 5.2 copy-start.21
  7.2 5.4 copy-start.25
  7.2 5.4 copy-start.26
  7.2 5.4 copy-start.27
  7.2 5.4 copy-start.28
  7.2 5.4 copy-start.29
  7.3 5.4 copy-start.30
  7.3 5.4 copy-start.22
  7.3 49.9 %all-gather.15.cloned.1.call-start = ((), (), s32[]{:S(2)}) async-start(), calls=%async_computation.7 | async-start | bytes 3932160 | tf_op jit(solution)/shard_map/all_gather | solution.py:97
  9.7 75.8 %all-gather.21.cloned.1.call-start = ((), (), s32[]{:S(2)}) async-start(), calls=%async_computation.10 | async-start | bytes 1310720 | tf_op jit(solution)/shard_map/all_gather | solution.py:98
  10.5 123.2 %all-gather.19.cloned.1.call-start = ((), (), s32[]{:S(2)}) async-start(), calls=%async_computation.9 | async-start | bytes 2621440 | tf_op jit(solution)/shard_map/all_gather | solution.py:127
  12.5 48.8 %copy-start.10 = (f32[512,8]{0,1:T(8,128)}, f32[512,8]{0,1:T(8,128)S(1)}, u32[]{:S(2)}) copy-start(f32[512,8]{0,1:T(8,128)S(1)} %get-tuple-element.171) | copy-start | bytes 49156
  12.6 48.8 %copy-start.12 = (f32[512,8]{0,1:T(8,128)}, f32[512,8]{0,1:T(8,128)S(1)}, u32[]{:S(2)}) copy-start(f32[512,8]{0,1:T(8,128)S(1)} %get-tuple-element.172) | copy-start | bytes 49156
  31.2 29.9 %copy-start.14 = (f32[1,1024]{1,0:T(1,128)}, f32[1,1024]{1,0:T(1,128)S(1)}, u32[]{:S(2)}) copy-start(f32[1,1024]{1,0:T(1,128)S(1)} %get-tuple-element.161) | copy-start | bytes 12292
  31.2 29.9 %copy-start.18 = (f32[1,1024]{1,0:T(1,128)}, f32[1,1024]{1,0:T(1,128)S(1)}, u32[]{:S(2)}) copy-start(f32[1,1024]{1,0:T(1,128)S(1)} %get-tuple-element.162) | copy-start | bytes 12292
  61.1 2.1 copy-start.6
  61.3 1.1 copy-start.5
  61.3 6.1 copy-start.20
  61.3 24.2 %copy-start.1 = (f32[1,512,1024]{2,1,0:T(8,128)S(1)}, f32[1,512,1024]{2,1,0:T(8,128)}, u32[]{:S(2)}) copy-start(f32[1,512,1024]{2,1,0:T(8,128)} %param.31) | copy-start | bytes 6291460
  64.1 116.3 %all-gather.17.cloned.1.call-start = ((), (), s32[]{:S(2)}) async-start(), calls=%async_computation.8 | async-start | bytes 2621440 | tf_op jit(solution)/shard_map/all_gather | solution.py:128
  66.2 201.3 %all-gather.23.cloned.1.call-start = ((), (), s32[]{:S(2)}) async-start(), calls=%async_computation.11 | async-start | bytes 5242880 | tf_op jit(solution)/shard_map/all_gather | solution.py:99
  66.8 221.0 %all-gather.25.cloned.1.call-start = ((), (), s32[]{:S(2)}) async-start(), calls=%async_computation.12 | async-start | bytes 5242880 | tf_op jit(solution)/shard_map/all_gather | solution.py:100
  67.4 367.3 %reduce-scatter.12.cloned.1.call-start = ((), (), s32[]{:S(2)}) async-start(), calls=%async_computation.13 | async-start | bytes 10485760 | tf_op jit(solution)/shard_map/reduce_scatter | solution.py:214
  149.6 20.5 %copy-start = (f32[8,512,2048]{2,1,0:T(8,128)S(1)}, f32[8,512,2048]{2,1,0:T(8,128)}, u32[]{:S(2)}) copy-start(f32[8,512,2048]{2,1,0:T(8,128)} %get-tuple-element.176) | copy-start | bytes 100663296
  179.5 13.3 copy-start.4
  192.7 25.3 %copy-start.8 = (bf16[512,8,8]{0,2,1:T(8,128)(2,1)S(1)}, bf16[512,8,8]{0,2,1:T(8,128)(2,1)}, u32[]{:S(2)}) copy-start(bf16[512,8,8]{0,2,1:T(8,128)(2,1)} %get-tuple-element.147) | copy-start | bytes 196612
  192.7 25.3 %copy-start.9 = (bf16[512,8,8]{0,2,1:T(8,128)(2,1)S(1)}, bf16[512,8,8]{0,2,1:T(8,128)(2,1)}, u32[]{:S(2)}) copy-start(bf16[512,8,8]{0,2,1:T(8,128)(2,1)} %get-tuple-element.148) | copy-start | bytes 196612
  258.7 0.7 copy-start.23
  258.7 8.8 copy-start.3
  258.8 361.2 %reduce-scatter.18.cloned.1.call-start = ((), (), s32[]{:S(2)}) async-start(), calls=%async_computation.17 | async-start | bytes 8912896 | tf_op jit(solution)/shard_map/reduce_scatter | solution.py:258
  295.2 1.3 copy-start.32
  302.4 499.7 %reduce-scatter.20.cloned.1.call-start = ((), (), s32[]{:S(2)}) async-start(), calls=%async_computation.19 | async-start | bytes 8912896 | tf_op jit(solution)/shard_map/reduce_scatter | solution.py:259
  309.7 526.0 %all-reduce.4.cloned.1.call-start = ((), (), s32[]{:S(2)}) async-start(), calls=%async_computation.23 | async-start | bytes 12582912 | tf_op jit(solution)/shard_map/psum | solution.py:157
  310.2 6.7 copy-start.24
  310.2 6.7 copy-start.33
  339.6 101.9 %copy-start.11 = (f32[512,8]{0,1:T(8,128)S(1)}, f32[512,8]{0,1:T(8,128)}, u32[]{:S(2)}) copy-start(f32[512,8]{0,1:T(8,128)} %copy-done.10) | copy-start | bytes 49156
  339.6 101.9 %copy-start.13 = (f32[512,8]{0,1:T(8,128)S(1)}, f32[512,8]{0,1:T(8,128)}, u32[]{:S(2)}) copy-start(f32[512,8]{0,1:T(8,128)} %copy-done.12) | copy-start | bytes 49156
  456.5 0.7 copy-start.15
  456.5 0.7 copy-start.19
  456.6 520.9 %reduce-scatter.14.cloned.1.call-start = ((), (), s32[]{:S(2)}) async-start(), calls=%async_computation.14 | async-start | bytes 6684672 | tf_op jit(solution)/shard_map/reduce_scatter | solution.py:256
  463.8 598.7 %reduce-scatter.16.cloned.1.call-start = ((), (), s32[]{:S(2)}) async-start(), calls=%async_computation.16 | async-start | bytes 2228224 | tf_op jit(solution)/shard_map/reduce_scatter | solution.py:257
  467.0 670.9 %reduce-scatter.24.cloned.1.call-start = ((), (), s32[]{:S(2)}) async-start(), calls=%async_computation.22 | async-start | bytes 278528
  470.0 711.7 %all-gather.29.cloned.1.call-start = ((), (), s32[]{:S(2)}) async-start(), calls=%async_computation.18 | async-start | bytes 2621440 | tf_op jit(solution)/shard_map/all_gather | solution.py:267
  620.0 607.8 %all-gather.31.cloned.1.call-start = ((), (), s32[]{:S(2)}) async-start(), calls=%async_computation.20 | async-start | bytes 2621440 | tf_op jit(solution)/shard_map/all_gather | solution.py:268
  802.2 175.4 %copy-start.31 = (u32[32]{0:T(128)S(1)}, u32[32]{0:T(128)}, u32[]{:S(2)}) copy-start(u32[32]{0:T(128)} %constant.141) | copy-start | bytes 388
  802.2 504.0 %reduce-scatter.22.cloned.1.call-start = ((), (), s32[]{:S(2)}) async-start(), calls=%async_computation.21 | async-start | bytes 557056
  839.1 391.6 %copy-start.16 = (f32[1,1024]{1,0:T(1,128)S(1)}, f32[1,1024]{1,0:T(1,128)}, u32[]{:S(2)}) copy-start(f32[1,1024]{1,0:T(1,128)} %get-tuple-element.159) | copy-start | bytes 12292
  839.1 391.6 %copy-start.17 = (f32[1,1024]{1,0:T(1,128)S(1)}, f32[1,1024]{1,0:T(1,128)}, u32[]{:S(2)}) copy-start(f32[1,1024]{1,0:T(1,128)} %get-tuple-element.160) | copy-start | bytes 12292
  840.2 501.1 %all-gather.27.cloned.1.call-start = ((), (), s32[]{:S(2)}) async-start(), calls=%async_computation.15 | async-start | bytes 1966080 | tf_op jit(solution)/shard_map/all_gather | solution.py:265
  1235.6 108.4 %copy-start.7 = (f32[256,2048]{1,0:T(8,128)S(1)}, f32[256,2048]{1,0:T(8,128)}, u32[]{:S(2)}) copy-start(f32[256,2048]{1,0:T(8,128)} %all-gather.29.cloned.1.call-done) | copy-start | bytes 6291460
Sparse Core Ops, SparseCore 0:
  10.5 46.6 all-gather.14
  59.0 26.4 all-gather.20
  87.7 45.9 all-gather.18
  135.6 44.6 all-gather.16
  182.0 51.4 all-gather.22
  235.2 52.6 all-gather.24
  290.2 144.4 reduce-scatter.11
  436.9 183.0 reduce-scatter.17
  622.3 179.8 reduce-scatter.19
  805.9 29.7 all-reduce.3
  838.1 139.3 reduce-scatter.13
  980.3 82.1 reduce-scatter.15
  1064.8 73.0 reduce-scatter.23
  1139.3 42.3 all-gather.28
  1183.1 44.6 all-gather.30
  1230.5 75.7 reduce-scatter.21
  1307.7 33.5 all-gather.26
where the time goes:
time: 1360 us; the launch traced here: 1350 us
  waiting for transfers between devices  942 us (69%)
  matrix products  161 us (12%)
  blocking collectives  126 us (9%)
  local copies, waits for them, and re-layouts  54.5 us (4%)
  other arithmetic  52.6 us (4%)
  between operations  15.4 us (1%)
    reduce_scatter x1, waiting for transfers between devices, local(): lax.psum_scatter(grad_down_w, ('fsdp', 'ctx'), scatter_dimension=1, tiled...  182 us
    reduce_scatter x1, waiting for transfers between devices, local(): lax.psum_scatter(grad_up_w, ('fsdp', 'ctx'), scatter_dimension=0, tiled=T...  150 us
    reduce_scatter x1, waiting for transfers between devices, local(): lax.psum_scatter(grad_joint_w, ('fsdp', 'ctx'), scatter_dimension=0, tile...  137 us
    unnamed x19, waiting for transfers between devices  130 us
    reduce_scatter x1, waiting for transfers between devices, local(): lax.psum_scatter(jnp.concatenate([key_part.reshape(count_rows * lax.axis_...  95.1 us
    all_gather x1, waiting for transfers between devices, local(): lax.all_gather(share_down, 'ctx', axis=1, tiled=True)  46.1 us
    all_gather x1, waiting for transfers between devices, local(): lax.all_gather(keys_here, 'ctx', axis=0, tiled=True)  44.2 us
    unnamed x1, blocking collectives  39.4 us
  transfers between devices with their start and end apart: 17, of which 16 were waited for; matrix products, arithmetic and copies ran while one was open for 19% of the time, Pallas kernels for 0%

commit v1 on v0

--- a/solution.py
+++ b/solution.py
@@ -7,6 +7,22 @@
 ROT = 16
 EPS = 1e-05
 ROPE_BASE = 10000.0
+
+
+def rates_mark(tile_in, dim_no):
+    bus_axis = "ctx"
+    q_next, r_now, tmp = (lax.axis_size(bus_axis), lax.axis_index(bus_axis), tile_in.shape[dim_no])
+    by_place = tuple(((to_i, (to_i + 1) % q_next) for to_i in range(q_next)))
+    x_new = jnp.zeros(
+        (*tile_in.shape[:dim_no], q_next * tmp, *tile_in.shape[dim_no + 1 :]), tile_in.dtype
+    )
+    all_rows = tile_in
+    for w in range(q_next):
+        h_now = (r_now - w) % q_next
+        x_new = lax.dynamic_update_slice_in_dim(x_new, all_rows, h_now * tmp, axis=dim_no)
+        if w < q_next - 1:
+            all_rows = lax.ppermute(all_rows, bus_axis, by_place)
+    return x_new
 
 
 def rope_tables(offsets):
@@ -265,7 +281,7 @@
         lax.all_gather(share_joint, "ctx", axis=0, tiled=True),
         lax.all_gather(share_output, "ctx", axis=1, tiled=True),
         lax.all_gather(share_up, "ctx", axis=0, tiled=True),
-        lax.all_gather(share_down, "ctx", axis=1, tiled=True),
+        rates_mark(share_down, 1),
         lax.all_gather(share_small, "ctx", axis=1, tiled=True),
         lax.all_gather(share_jbias, "ctx", axis=1, tiled=True),
         lax.all_gather(share_upbias, "ctx", axis=0, tiled=True),

time: 1360 us -> 1320 us (0.971)
  waiting for transfers between devices: 942 us -> 854 us
  local copies, waits for them, and re-layouts: 54.5 us -> 87.3 us
    all_gather x1 -> x0, waiting for transfers between devices: 46.1 us -> none  [local(): lax.all_gather(share_down, 'ctx', axis=1, tiled=True)]
    unnamed x19 -> x18, waiting for transfers between devices: 130 us -> 99.9 us
    dynamic_update_slice x0 -> x4, local copies, waits for them, and re-layouts: none -> 24.8 us  [rates_mark(): lax.dynamic_update_slice_in_dim(x_new, all_rows, h_now * tmp, axis=dim_no)]
    ppermute x0 -> x3, waiting for transfers between devices: none -> 15.5 us  [rates_mark(): all_rows = lax.ppermute(all_rows, bus_axis, by_place)]
    psum x1, waiting for transfers between devices: 33.3 us -> 17.9 us  [local(): mixed_all = lax.psum(partial_value, 'tp')]
  transfers between devices with their start and end apart: 17 -> 19, of which waited for: 16 -> 16; matrix products, arithmetic and copies ran while one was open for 19% -> 22% of each run, Pallas kernels for 0% -> 0%
where the time goes in v1:
time: 1320 us; the launch traced here: 1310 us
  waiting for transfers between devices  854 us (65%)
  matrix products  161 us (12%)
  blocking collectives  138 us (10%)
  local copies, waits for them, and re-layouts  87.3 us (7%)
  other arithmetic  52.6 us (4%)
  between operations  15.5 us (1%)
    reduce_scatter x1, waiting for transfers between devices, local(): lax.psum_scatter(grad_down_w, ('fsdp', 'ctx'), scatter_dimension=1, tiled...  182 us
    reduce_scatter x1, waiting for transfers between devices, local(): lax.psum_scatter(grad_up_w, ('fsdp', 'ctx'), scatter_dimension=0, tiled=T...  150 us
    reduce_scatter x1, waiting for transfers between devices, local(): lax.psum_scatter(grad_joint_w, ('fsdp', 'ctx'), scatter_dimension=0, tile...  137 us
    unnamed x18, waiting for transfers between devices  99.9 us
    reduce_scatter x1, waiting for transfers between devices, local(): lax.psum_scatter(jnp.concatenate([key_part.reshape(count_rows * lax.axis_...  95 us
    unnamed x1, blocking collectives  50.5 us
    all_gather x1, waiting for transfers between devices, local(): lax.all_gather(keys_here, 'ctx', axis=0, tiled=True)  44.2 us
    all_gather x1, waiting for transfers between devices, local(): lax.all_gather(share_up, 'ctx', axis=0, tiled=True)  30.2 us
  transfers between devices with their start and end apart: 19, of which 16 were waited for; matrix products, arithmetic and copies ran while one was open for 22% of the time, Pallas kernels for 0%

profile of v1, /device:TPU:0, one launch (start us, length us, event | category | flops | bytes accessed | tf_op | source)
XLA Modules:
  0.0 1309.6 jit_solution(13507901342852622025)
XLA Ops:
  7.3 2.4 copy.57
  12.7 9.5 all_gather.54
  22.3 8.3 all_gather.52
  31.2 26.0 %all-gather.14.cloned.1.call-done = bf16[1024,3,512]{0,2,1:T(8,128)(2,1)} async-done(((bf16[256,3,512]{0,2,1:T(8,128)(2,1)}), bf16[1024,3,512]{0,2,1:T(8,128)(2,1)}) %all-gather.14.cloned.1.call-update) | async-done | bytes 3145744 | tf_op jit(solution)/shard_map/all_gather | solution.py:113
  57.2 3.9 convolution_add_fusion
  67.5 11.9 all-gather
  80.6 4.9 all-gather.20.cloned.1.call-done
  85.5 2.8 fusion.75
  89.5 44.2 %all-gather.18.cloned.1.call-done = bf16[2048,8,64]{0,2,1:T(8,128)(2,1)} async-done(((bf16[512,8,64]{0,2,1:T(8,128)(2,1)}), bf16[2048,8,64]{0,2,1:T(8,128)(2,1)}) %all-gather.18.cloned.1.call-update) | async-done | bytes 2097168 | tf_op jit(solution)/shard_map/all_gather | solution.py:143
  133.6 16.0 %fusion = (f32[8,512]{1,0:T(8,128)S(1)}, f32[8,512,2048]{2,1,0:T(8,128)}) fusion(pred[512,2048]{1,0:T(8,128)(4,1)S(1)} %fusion.7, bf16[2048,8,64]{0,2,1:T(8,128)(2,1)} %all-gather.18.cloned.1.call-done, bf16[512,8,48]{0,2,1:T(8,128)(2,1)S(1)} %slice.170, bf16[512,8,8]{0,2,1:T(8,128)(2,1)} %get-tuple-element.148, bf16[512,8,8]{0,2,1:T(8,128)(2,1)} %get-tuple-element.147), kind=kOutput, calls=%fused_computation.4 | convolution fusion | flops 1100476416 | bytes 37240832 | tf_op jit(solution)/shard_map/while/body/eval_jaxpr/qhe,khe->hqk/dot_general | solution.py:71
  149.6 15.9 %exponential_reduce_fusion = f32[8,512]{1,0:T(8,128)S(1)} fusion(f32[8,512,2048]{2,1,0:T(8,128)} %get-tuple-element.176, f32[8,512]{1,0:T(8,128)S(1)} %get-tuple-element.175, pred[512,2048]{1,0:T(8,128)(4,1)S(1)} %fusion.7), kind=kLoop, calls=%fused_computation.2 | loop fusion | flops 33550336 | bytes 34635776 | tf_op jit(solution)/shard_map/while/body/eval_jaxpr/reduce_sum | solution.py:160
  165.5 4.6 copy-done
  170.1 9.4 exponential_convert_fusion
  180.3 12.4 multiply_reduce_fusion.2
  192.7 25.3 %multiply_convert_fusion = bf16[8,512,2048]{2,1,0:T(8,128)(2,1)} fusion(bf16[8,512,2048]{2,1,0:T(8,128)(2,1)} %exponential_convert_fusion, bf16[512,8,64]{0,2,1:T(8,128)(2,1)S(1)} %bitcast.212, bf16[2048,8,64]{0,2,1:T(8,128)(2,1)} %all-gather.16.cloned.1.call-done, f32[8,512]{1,0:T(8,128)S(1)} %bitcast.227), kind=kOutput, calls=%fused_computation | convolution fusion | flops 1107296256 | bytes 36192256 | tf_op jit(solution)/shard_map/while/body/eval_jaxpr/qhe,khe->hqk/dot_general | solution.py:205
  218.1 10.9 convolution_multiply_fusion
  228.9 5.4 copy.58
  234.3 10.9 fusion.82
  245.2 5.4 copy.59
  250.6 8.2 pad_maximum_fusion
  259.4 8.0 all-gather.1
  267.5 15.1 %multiply_convert_fusion.1 = (bf16[512,2048]{1,0:T(8,128)(2,1)}, f32[512,2048]{1,0:T(8,128)}, f32[512,2048]{1,0:T(8,128)}) fusion(f32[2048]{0:T(1024)S(1)} %bitcast.253, bf16[1024,2048]{1,0:T(8,128)(2,1)} %all-gather.22.cloned.1.call-done, bf16[1,512,1024]{2,1,0:T(8,128)(2,1)S(1)} %copy-done.3, f32[1024]{0:T(1024)S(1)} %bitcast.257, f32[1024]{0:T(1024)S(1)} %bitcast.234, ...), kind=kOutput, calls=%fused_computation.9 | convolution fusion | flops 2219835392 | bytes 15749120 | tf_op jit(solution)/shard_map/dot_general | solution.py:168
  282.6 5.2 all-gather.24.cloned.1.call-done
  287.8 7.4 fusion.72
  296.6 5.8 fusion.46
  302.5 7.2 fusion.73
  310.2 6.7 fusion.81
  316.9 3.7 fusion.48
  320.6 12.7 fusion.41
  335.4 4.2 convolution_add_fusion.1
  339.6 95.0 %reduce-scatter.12.cloned.1.call-done = f32[512,1024]{1,0:T(8,128)} async-done(((f32[2048,1024]{1,0:T(8,128)}), f32[512,1024]{1,0:T(8,128)}) %reduce-scatter.12.cloned.1.call-update) | async-done | bytes 2097168 | tf_op jit(solution)/shard_map/reduce_scatter | solution.py:230
  434.6 3.0 fusion.68
  437.7 2.5 copy.60
  442.6 2.8 pad_maximum_fusion.2
  445.4 2.6 copy.61
  448.0 2.5 copy.62
  450.5 6.0 convolution_bitcast_fusion
  457.2 6.6 fusion.55
  463.9 3.1 fusion.43
  470.1 149.9 %reduce-scatter.18.cloned.1.call-done = f32[64,2048]{1,0:T(8,128)} async-done(((f32[1024,2048]{1,0:T(8,128)}), f32[64,2048]{1,0:T(8,128)}) %reduce-scatter.18.cloned.1.call-update) | async-done | bytes 524304 | tf_op jit(solution)/shard_map/reduce_scatter | solution.py:274
  620.1 182.1 %reduce-scatter.20.cloned.1.call-done = f32[2048,64]{0,1:T(8,128)} async-done(((f32[2048,1024]{0,1:T(8,128)}), f32[2048,64]{0,1:T(8,128)}) %reduce-scatter.20.cloned.1.call-update) | async-done | bytes 524304 | tf_op jit(solution)/shard_map/reduce_scatter | solution.py:275
  802.3 15.5 %collective-permute-done = f32[2048,64]{0,1:T(8,128)} collective-permute-done((f32[2048,64]{0,1:T(8,128)}, f32[2048,64]{0,1:T(8,128)}, u32[]{:S(2)}, u32[]{:S(2)}) %collective-permute-start) | collective-permute-done | bytes 524320 | tf_op jit(solution)/shard_map/ppermute | solution.py:24
  817.8 17.9 %all-reduce.4.cloned.1.call-done = (f32[512,1024]{1,0:T(8,128)}, f32[512,1024]{1,0:T(8,128)}, f32[512,1024]{1,0:T(8,128)}) async-done(((f32[512,1024]{1,0:T(8,128)}, f32[512,1024]{1,0:T(8,128)}, f32[512,1024]{1,0:T(8,128)}), (f32[512,1024]{1,0:T(8,128)}, f32[512,1024]{1,0:T(8,128)}, f32[512,1024]{1,0:T(8,128)})) %all-reduce.4.cloned.1.call-update) | async-done | bytes 6291472 | tf_op jit(solution)/shard_map/psum | solution.py:173
  835.7 3.4 fusion.35
  840.2 137.3 %reduce-scatter.14.cloned.1.call-done = f32[64,3,512]{2,0,1:T(8,128)} async-done(((f32[1024,3,512]{2,0,1:T(8,128)}), f32[64,3,512]{2,0,1:T(8,128)}) %reduce-scatter.14.cloned.1.call-update) | async-done | bytes 393232 | tf_op jit(solution)/shard_map/reduce_scatter | solution.py:272
  978.9 50.5 %all-reduce = f32[2048]{0:T(1024)S(1)} all-reduce(f32[2048]{0:T(1024)S(1)} %get-tuple-element.179), channel_id=9, replica_groups=mesh['fsdp'=4,'ctx'=4,'tp'=2] {'fsdp','ctx'}, use_global_device_ids=true, to_apply=%region_25.26.clone | all-reduce | flops 2048 | bytes 16384
  1029.5 8.2 all-gather.4
  1037.7 25.4 %reduce-scatter.16.cloned.1.call-done = f32[512,64]{0,1:T(8,128)} async-done(((f32[512,1024]{0,1:T(8,128)}), f32[512,64]{0,1:T(8,128)}) %reduce-scatter.16.cloned.1.call-update) | async-done | bytes 131088 | tf_op jit(solution)/shard_map/reduce_scatter | solution.py:273
  1063.1 15.9 %all_gather.65 = f32[512,256]{0,1:T(8,128)} all-gather(f32[512,64]{0,1:T(8,128)} %reduce-scatter.16.cloned.1.call-done), channel_id=1, replica_groups=mesh['fsdp'=4,'ctx'=4,'tp'=2] {'ctx'}, dimensions={1}, use_global_device_ids=true | all-gather | bytes 655360 | tf_op jit(solution)/shard_map/all_gather | solution.py:282
  1081.0 2.4 copy.67
  1084.8 6.1 dynamic_update_slice.25
  1093.3 6.3 dynamic_update_slice.26
  1099.6 2.4 copy.69
  1101.9 5.5 dynamic_update_slice.27
  1107.4 2.4 copy.70
  1109.8 6.9 dynamic_update_slice.28
  1116.7 24.4 %reduce-scatter.24.cloned.1.call-done = f32[32,3]{1,0:T(8,128)} async-done(((f32[512,3]{1,0:T(8,128)}), f32[32,3]{1,0:T(8,128)}) %reduce-scatter.24.cloned.1.call-update) | async-done | bytes 400
  1141.9 12.1 all-gather.3
  1154.7 30.2 %all-gather.28.cloned.1.call-done = f32[256,2048]{1,0:T(8,128)} async-done(((f32[64,2048]{1,0:T(8,128)}), f32[256,2048]{1,0:T(8,128)}) %all-gather.28.cloned.1.call-update) | async-done | bytes 2097168 | tf_op jit(solution)/shard_map/all_gather | solution.py:283
  1185.0 4.8 fusion.31
  1189.8 73.5 %reduce-scatter.22.cloned.1.call-done = f32[64,6]{1,0:T(8,128)} async-done(((f32[1024,6]{1,0:T(8,128)}), f32[64,6]{1,0:T(8,128)}) %reduce-scatter.22.cloned.1.call-update) | async-done | bytes 1552
  1264.1 13.4 %all-gather.2 = f32[4,64,6]{1,2,0:T(8,128)S(1)} all-gather(f32[1,64,6]{1,2,0:T(8,128)S(1)} %bitcast.243), channel_id=1, replica_groups=mesh['fsdp'=4,'ctx'=4,'tp'=2] {'ctx'}, dimensions={0}, use_global_device_ids=true | all-gather | bytes 7680 | tf_op jit(solution)/shard_map/all_gather | solution.py:285
  1278.2 20.2 %all-gather.26.cloned.1.call-done = f32[256,3,512]{2,0,1:T(8,128)} async-done(((f32[64,3,512]{2,0,1:T(8,128)}), f32[256,3,512]{2,0,1:T(8,128)}) %all-gather.26.cloned.1.call-update) | async-done | bytes 1572880 | tf_op jit(solution)/shard_map/all_gather | solution.py:281
  1298.4 2.7 copy.89
  (161 shorter events, 36.7 us)
Async XLA Ops:
  7.2 4.8 copy-start.2
  7.2 5.2 copy-start.21
  7.2 5.4 copy-start.25
  7.2 5.4 copy-start.26
  7.2 5.4 copy-start.27
  7.2 5.4 copy-start.28
  7.2 5.4 copy-start.29
  7.3 5.4 copy-start.30
  7.3 5.4 copy-start.22
  7.3 49.9 %all-gather.14.cloned.1.call-start = ((), (), s32[]{:S(2)}) async-start(), calls=%async_computation.7 | async-start | bytes 3932160 | tf_op jit(solution)/shard_map/all_gather | solution.py:113
  9.7 75.8 %all-gather.20.cloned.1.call-start = ((), (), s32[]{:S(2)}) async-start(), calls=%async_computation.10 | async-start | bytes 1310720 | tf_op jit(solution)/shard_map/all_gather | solution.py:114
  10.5 123.2 %all-gather.18.cloned.1.call-start = ((), (), s32[]{:S(2)}) async-start(), calls=%async_computation.9 | async-start | bytes 2621440 | tf_op jit(solution)/shard_map/all_gather | solution.py:143
  12.5 48.8 %copy-start.10 = (f32[512,8]{0,1:T(8,128)}, f32[512,8]{0,1:T(8,128)S(1)}, u32[]{:S(2)}) copy-start(f32[512,8]{0,1:T(8,128)S(1)} %get-tuple-element.171) | copy-start | bytes 49156
  12.6 48.8 %copy-start.12 = (f32[512,8]{0,1:T(8,128)}, f32[512,8]{0,1:T(8,128)S(1)}, u32[]{:S(2)}) copy-start(f32[512,8]{0,1:T(8,128)S(1)} %get-tuple-element.172) | copy-start | bytes 49156
  31.2 29.9 %copy-start.14 = (f32[1,1024]{1,0:T(1,128)}, f32[1,1024]{1,0:T(1,128)S(1)}, u32[]{:S(2)}) copy-start(f32[1,1024]{1,0:T(1,128)S(1)} %get-tuple-element.161) | copy-start | bytes 12292
  31.2 29.9 %copy-start.18 = (f32[1,1024]{1,0:T(1,128)}, f32[1,1024]{1,0:T(1,128)S(1)}, u32[]{:S(2)}) copy-start(f32[1,1024]{1,0:T(1,128)S(1)} %get-tuple-element.162) | copy-start | bytes 12292
  61.1 2.1 copy-start.6
  61.3 1.1 copy-start.5
  61.3 6.1 copy-start.20
  61.3 24.2 %copy-start.1 = (f32[1,512,1024]{2,1,0:T(8,128)S(1)}, f32[1,512,1024]{2,1,0:T(8,128)}, u32[]{:S(2)}) copy-start(f32[1,512,1024]{2,1,0:T(8,128)} %param.31) | copy-start | bytes 6291460
  64.1 116.3 %all-gather.16.cloned.1.call-start = ((), (), s32[]{:S(2)}) async-start(), calls=%async_computation.8 | async-start | bytes 2621440 | tf_op jit(solution)/shard_map/all_gather | solution.py:144
  66.2 201.3 %all-gather.22.cloned.1.call-start = ((), (), s32[]{:S(2)}) async-start(), calls=%async_computation.11 | async-start | bytes 5242880 | tf_op jit(solution)/shard_map/all_gather | solution.py:115
  66.8 221.0 %all-gather.24.cloned.1.call-start = ((), (), s32[]{:S(2)}) async-start(), calls=%async_computation.12 | async-start | bytes 5242880 | tf_op jit(solution)/shard_map/all_gather | solution.py:116
  67.4 367.3 %reduce-scatter.12.cloned.1.call-start = ((), (), s32[]{:S(2)}) async-start(), calls=%async_computation.13 | async-start | bytes 10485760 | tf_op jit(solution)/shard_map/reduce_scatter | solution.py:230
  149.6 20.5 %copy-start = (f32[8,512,2048]{2,1,0:T(8,128)S(1)}, f32[8,512,2048]{2,1,0:T(8,128)}, u32[]{:S(2)}) copy-start(f32[8,512,2048]{2,1,0:T(8,128)} %get-tuple-element.176) | copy-start | bytes 100663296
  179.5 13.3 %copy-start.4 = (bf16[512,512]{0,1:T(8,128)(2,1)S(1)}, bf16[512,512]{0,1:T(8,128)(2,1)}, u32[]{:S(2)}) copy-start(bf16[512,512]{0,1:T(8,128)(2,1)} %fusion.75) | copy-start | bytes 1572868
  192.7 25.3 %copy-start.8 = (bf16[512,8,8]{0,2,1:T(8,128)(2,1)S(1)}, bf16[512,8,8]{0,2,1:T(8,128)(2,1)}, u32[]{:S(2)}) copy-start(bf16[512,8,8]{0,2,1:T(8,128)(2,1)} %get-tuple-element.147) | copy-start | bytes 196612
  192.7 25.3 %copy-start.9 = (bf16[512,8,8]{0,2,1:T(8,128)(2,1)S(1)}, bf16[512,8,8]{0,2,1:T(8,128)(2,1)}, u32[]{:S(2)}) copy-start(bf16[512,8,8]{0,2,1:T(8,128)(2,1)} %get-tuple-element.148) | copy-start | bytes 196612
  258.7 0.7 copy-start.23
  258.7 8.8 copy-start.3
  258.8 361.2 %reduce-scatter.18.cloned.1.call-start = ((), (), s32[]{:S(2)}) async-start(), calls=%async_computation.17 | async-start | bytes 8912896 | tf_op jit(solution)/shard_map/reduce_scatter | solution.py:274
  295.2 1.4 copy-start.32
  302.5 499.7 %reduce-scatter.20.cloned.1.call-start = ((), (), s32[]{:S(2)}) async-start(), calls=%async_computation.19 | async-start | bytes 8912896 | tf_op jit(solution)/shard_map/reduce_scatter | solution.py:275
  309.8 525.9 %all-reduce.4.cloned.1.call-start = ((), (), s32[]{:S(2)}) async-start(), calls=%async_computation.22 | async-start | bytes 12582912 | tf_op jit(solution)/shard_map/psum | solution.py:173
  310.2 6.7 copy-start.24
  310.2 6.7 copy-start.33
  339.6 101.8 %copy-start.11 = (f32[512,8]{0,1:T(8,128)S(1)}, f32[512,8]{0,1:T(8,128)}, u32[]{:S(2)}) copy-start(f32[512,8]{0,1:T(8,128)} %copy-done.10) | copy-start | bytes 49156
  339.6 101.8 %copy-start.13 = (f32[512,8]{0,1:T(8,128)S(1)}, f32[512,8]{0,1:T(8,128)}, u32[]{:S(2)}) copy-start(f32[512,8]{0,1:T(8,128)} %copy-done.12) | copy-start | bytes 49156
  456.5 0.7 copy-start.15
  456.5 0.7 copy-start.19
  456.6 521.0 %reduce-scatter.14.cloned.1.call-start = ((), (), s32[]{:S(2)}) async-start(), calls=%async_computation.14 | async-start | bytes 6684672 | tf_op jit(solution)/shard_map/reduce_scatter | solution.py:272
  463.8 599.3 %reduce-scatter.16.cloned.1.call-start = ((), (), s32[]{:S(2)}) async-start(), calls=%async_computation.16 | async-start | bytes 2228224 | tf_op jit(solution)/shard_map/reduce_scatter | solution.py:273
  467.0 674.1 %reduce-scatter.24.cloned.1.call-start = ((), (), s32[]{:S(2)}) async-start(), calls=%async_computation.21 | async-start | bytes 278528
  470.0 714.9 %all-gather.28.cloned.1.call-start = ((), (), s32[]{:S(2)}) async-start(), calls=%async_computation.18 | async-start | bytes 2621440 | tf_op jit(solution)/shard_map/all_gather | solution.py:283
  620.0 357.7 %copy-start.31 = (u32[32]{0:T(128)S(1)}, u32[32]{0:T(128)}, u32[]{:S(2)}) copy-start(u32[32]{0:T(128)} %constant.180) | copy-start | bytes 388
  620.0 643.3 %reduce-scatter.22.cloned.1.call-start = ((), (), s32[]{:S(2)}) async-start(), calls=%async_computation.20 | async-start | bytes 557056
  802.1 15.6 %collective-permute-start = (f32[2048,64]{0,1:T(8,128)}, f32[2048,64]{0,1:T(8,128)}, u32[]{:S(2)}, u32[]{:S(2)}) collective-permute-start(f32[2048,64]{0,1:T(8,128)} %reduce-scatter.20.cloned.1.call-done), channel_id=1, source_target_pairs={{0,2},{2,4},{4,6},{6,0},{1,3},{3,5},{5,7},{7,1},{8,10},{10,12},{12... | collective-permute-start | bytes 1572872 | tf_op jit(solution)/shard_map/ppermute | solution.py:24
  817.8 159.8 %collective-permute-start.1 = (f32[2048,64]{0,1:T(8,128)}, f32[2048,64]{0,1:T(8,128)}, u32[]{:S(2)}, u32[]{:S(2)}) collective-permute-start(f32[2048,64]{0,1:T(8,128)} %collective-permute-done), channel_id=1, source_target_pairs={{0,2},{2,4},{4,6},{6,0},{1,3},{3,5},{5,7},{7,1},{8,10},{10,12},{12... | collective-permute-start | bytes 1572872 | tf_op jit(solution)/shard_map/ppermute | solution.py:24
  840.2 458.2 %all-gather.26.cloned.1.call-start = ((), (), s32[]{:S(2)}) async-start(), calls=%async_computation.15 | async-start | bytes 1966080 | tf_op jit(solution)/shard_map/all_gather | solution.py:281
  977.5 129.9 %collective-permute-start.2 = (f32[2048,64]{0,1:T(8,128)}, f32[2048,64]{0,1:T(8,128)}, u32[]{:S(2)}, u32[]{:S(2)}) collective-permute-start(f32[2048,64]{0,1:T(8,128)} %collective-permute-done.1), channel_id=1, source_target_pairs={{0,2},{2,4},{4,6},{6,0},{1,3},{3,5},{5,7},{7,1},{8,10},{10,12},{12... | collective-permute-start | bytes 1572872 | tf_op jit(solution)/shard_map/ppermute | solution.py:24
  1099.6 85.4 %copy-start.16 = (f32[1,1024]{1,0:T(1,128)S(1)}, f32[1,1024]{1,0:T(1,128)}, u32[]{:S(2)}) copy-start(f32[1,1024]{1,0:T(1,128)} %get-tuple-element.159) | copy-start | bytes 12292
  1099.6 85.4 %copy-start.17 = (f32[1,1024]{1,0:T(1,128)S(1)}, f32[1,1024]{1,0:T(1,128)}, u32[]{:S(2)}) copy-start(f32[1,1024]{1,0:T(1,128)} %get-tuple-element.160) | copy-start | bytes 12292
  1189.8 111.2 %copy-start.7 = (f32[256,2048]{1,0:T(8,128)S(1)}, f32[256,2048]{1,0:T(8,128)}, u32[]{:S(2)}) copy-start(f32[256,2048]{1,0:T(8,128)} %all-gather.28.cloned.1.call-done) | copy-start | bytes 6291460
Sparse Core Ops, SparseCore 0:
  10.5 46.6 all-gather.13
  59.0 26.4 all-gather.19
  87.7 45.9 all-gather.17
  135.6 44.6 all-gather.15
  182.0 51.4 all-gather.21
  235.2 52.6 all-gather.23
  290.2 144.4 reduce-scatter.11
  436.9 183.0 reduce-scatter.17
  622.3 179.8 reduce-scatter.19
  805.9 29.7 all-reduce.3
  838.1 139.3 reduce-scatter.13
  980.3 82.7 reduce-scatter.15
  1065.4 75.6 reduce-scatter.23
  1142.6 42.3 all-gather.27
  1187.6 75.6 reduce-scatter.21
  1264.8 33.4 all-gather.25
